TPU v7x, 256 devices: a whole 4x4x8 slice. The times are simulated.
256 devices in a mesh: line: 8 (over z_lo, core), bus: 32 (over y, x, z_hi).
Axes of the slice: x: 4, y: 4, z: 8 (z_hi: 2, z_lo: 4; z = z_hi * 4 + z_lo), core: 2. Of those that a mesh axis runs over, the one named last changes fastest.
Arguments:
- injections: float32 [64, 69632], P(None, 'bus'), may hold values from -6 to 6
- transfer_factors: float32 [4096, 69632], P('line', 'bus'), may hold values from -0.0234375 to 0.0234375
- outage_factors: float32 [4096, 8192], P('line', 'bus'), may hold values from -1 to 1
- outage_line: int32 [8192], P('bus'), may hold values from 0 to 4095
- limit_table: int32 [4, 4096], P(None, 'line'), may hold values from 1 to 4
- scenario_tier: int32 [64], replicated, may hold values from 0 to 3
Outputs:
- injection_grad: float32 [64, 69632], P('line', 'bus')
- mean_penalty: float32 [64], replicated
All inputs are finite; a program needn't handle non-finite values.
Results may differ from a plain program's by a relative error of at most 0.0003.
Values sent between devices are 32-bit elements; how exact they have to be, the bound alone decides.
A program may use at most 64 MiB of HBM per device.

v0:
```python
import math
import jax
import jax.numpy as jnp
from jax import lax
from jax.sharding import PartitionSpec as P

LINES = 4096
OUTAGES = 8192


def body(injections, transfer_factors, outage_factors, outage_line, limit_table, scenario_tier):
    scenarios = injections.shape[0]
    line_rows = transfer_factors.shape[0]
    outage_cols = outage_factors.shape[1]
    partial_flows = jnp.dot(
        injections,
        transfer_factors.T,
        precision=lax.Precision.HIGHEST,
        preferred_element_type=jnp.float32,
    )
    line_flows = lax.psum(partial_flows, "bus")
    line_start = lax.axis_index("line") * line_rows
    local_index = outage_line - line_start
    selector = (local_index[None, :] == jnp.arange(line_rows, dtype=jnp.int32)[:, None]).astype(
        jnp.float32
    )
    every_flow = lax.all_gather(line_flows, "line", axis=1, tiled=True)
    outage_flows = jnp.take(every_flow, outage_line, axis=1)
    tier_onehot = (
        scenario_tier[:, None] == jnp.arange(limit_table.shape[0], dtype=jnp.int32)[None, :]
    ).astype(jnp.float32)
    limits = 0.4 * jnp.dot(
        tier_onehot,
        limit_table.astype(jnp.float32),
        precision=lax.Precision.HIGHEST,
        preferred_element_type=jnp.float32,
    )
    block_rows = math.gcd(scenarios, 16)
    num_blocks = scenarios // block_rows

    def one_block(values):
        flow_block, outage_block, limit_block = values
        post = flow_block[:, :, None] + outage_factors[None, :, :] * outage_block[:, None, :]
        excess = jnp.maximum(jnp.abs(post) - limit_block[:, :, None], 0.0)
        weight = 2.0 * excess * jnp.sign(post) / OUTAGES
        return (
            jnp.sum(excess * excess, axis=(1, 2)),
            jnp.sum(weight, axis=2),
            jnp.sum(weight * outage_factors[None, :, :], axis=1),
        )

    penalty, direct, back_part = lax.map(
        one_block,
        (
            line_flows.reshape(num_blocks, block_rows, line_rows),
            outage_flows.reshape(num_blocks, block_rows, outage_cols),
            limits.reshape(num_blocks, block_rows, line_rows),
        ),
    )
    penalty = penalty.reshape(scenarios)
    direct = direct.reshape(scenarios, line_rows)
    back_part = back_part.reshape(scenarios, outage_cols)
    back = lax.psum(back_part, "line")
    carried = jnp.dot(
        back, selector.T, precision=lax.Precision.HIGHEST, preferred_element_type=jnp.float32
    )
    flow_grad, penalty_sum = lax.psum((direct + carried, penalty), "bus")
    total_penalty = lax.psum(penalty, ("line", "bus"))
    mean_penalty = total_penalty / (LINES * OUTAGES)
    injection_grad = lax.psum_scatter(
        jnp.dot(
            flow_grad,
            transfer_factors,
            precision=lax.Precision.HIGHEST,
            preferred_element_type=jnp.float32,
        ),
        "line",
        scatter_dimension=0,
        tiled=True,
    )
    return (injection_grad, mean_penalty)


def solution(mesh):
    return jax.shard_map(
        body,
        mesh=mesh,
        in_specs=(
            P(None, "bus"),
            P("line", "bus"),
            P("line", "bus"),
            P("bus"),
            P(None, "line"),
            P(),
        ),
        out_specs=(P("line", "bus"), P()),
        check_vma=False,
    )
```

profile of v0, /device:TPU:1, one launch (start us, length us, event | category | flops | bytes accessed | tf_op | source)
XLA Modules:
  0.0 1058.1 jit_solution(12316503134355533745)
XLA Ops:
  7.2 0.0 copy-start
  7.2 0.0 copy-start.3
  7.2 0.0 copy-start.2
  7.2 0.0 copy-start.4
  7.2 0.0 copy-start.1
  7.2 0.0 all-reduce.6.cloned.1.call-start
  7.3 1.0 copy-done
  8.2 7.2 fusion.3
  15.5 0.0 all-reduce.6.cloned.1.call-update
  15.5 0.0 all-gather.2.cloned.1.call-start
  15.5 387.3 %all-reduce.6.cloned.1.call-done = f32[64,512]{1,0:T(8,128)} async-done(((f32[64,512]{1,0:T(8,128)}), f32[64,512]{1,0:T(8,128)}) %all-reduce.6.cloned.1.call-update) | async-done | bytes 131088 | tf_op jit(solution)/shard_map/psum | solution.py:21
  402.9 0.0 all-gather.2.cloned.1.call-update
  402.9 0.0 all-reduce.8.cloned.1.call-start
  403.0 0.0 copy-done.3
  403.0 0.0 copy-done.2
  403.0 0.0 copy-done.4
  403.0 0.3 convolution_multiply_fusion
  403.3 49.7 %all-gather.2.cloned.1.call-done = f32[64,4096]{1,0:T(8,128)} async-done(((f32[64,512]{1,0:T(8,128)}), f32[64,4096]{1,0:T(8,128)}) %all-gather.2.cloned.1.call-update) | async-done | bytes 1048592 | tf_op jit(solution)/shard_map/all_gather | solution.py:27
  453.0 1.8 copy.14
  454.8 0.7 gather_fusion
  455.6 0.1 copy.15
  455.7 0.0 copy-done.1
  455.7 40.5 %while.14 = (s32[]{:T(128)}, f32[4,16]{1,0:T(4,128)S(1)}, f32[4,16,512]{2,1,0:T(8,128)}, f32[4,16,256]{2,1,0:T(8,128)}, f32[4,16,512]{2,1,0:T(8,128)}, /*index=5...) while((s32[]{:T(128)}, f32[4,16]{1,0:T(4,128)S(1)}, ...), condition=%wide.region_5.6_spmd, body=%wide.region_1.5_spmd.sunk | while | flops 29478896 | bytes 2491697 | solution.py:52
  455.7 0.8 dynamic-slice_bitcast_fusion.5
  456.5 8.0 multiply_reduce_fusion.4
  464.5 0.6 bitcast_dynamic-update-slice_fusion.4
  465.2 0.6 bitcast_dynamic-update-slice_fusion.5
  465.8 0.8 dynamic-slice_bitcast_fusion.5
  466.6 8.0 multiply_reduce_fusion.4
  474.7 0.6 bitcast_dynamic-update-slice_fusion.4
  475.3 0.6 bitcast_dynamic-update-slice_fusion.5
  475.9 0.8 dynamic-slice_bitcast_fusion.5
  476.7 8.0 multiply_reduce_fusion.4
  484.8 0.6 bitcast_dynamic-update-slice_fusion.4
  485.4 0.6 bitcast_dynamic-update-slice_fusion.5
  486.0 0.8 dynamic-slice_bitcast_fusion.5
  486.8 8.0 multiply_reduce_fusion.4
  494.9 0.6 bitcast_dynamic-update-slice_fusion.4
  495.5 0.6 bitcast_dynamic-update-slice_fusion.5
  496.1 0.0 copy-start.5
  496.1 0.0 all-reduce.8.cloned.1.call-update
  496.2 0.0 all-reduce.10.cloned.1.call-start
  496.2 68.3 %all-reduce.8.cloned.1.call-done = f32[64,256]{1,0:T(8,128)} async-done(((f32[64,256]{1,0:T(8,128)}), f32[64,256]{1,0:T(8,128)}) %all-reduce.8.cloned.1.call-update) | async-done | bytes 65552 | tf_op jit(solution)/shard_map/psum | solution.py:63
  564.5 2.0 convolution_add_fusion
  566.5 0.0 all-reduce.10.cloned.1.call-update
  566.5 0.0 all-reduce.12.cloned.1.call-start
  566.6 385.1 %all-reduce.10.cloned.1.call-done = f32[64,512]{1,0:T(8,128)} async-done(((f32[64,512]{1,0:T(8,128)}), f32[64,512]{1,0:T(8,128)}) %all-reduce.10.cloned.1.call-update) | async-done | bytes 131088 | tf_op jit(solution)/shard_map/psum | solution.py:67
  951.6 5.9 fusion.4
  957.6 0.0 all-reduce.12.cloned.1.call-update
  957.6 0.0 copy-done.5
  957.6 0.6 dynamic-slice
  958.8 0.1 reshape.44
  958.9 90.6 %psum.31 = f32[64]{0:T(128)S(1)} all-reduce(f32[64]{0:T(128)S(1)} %reshape.44), channel_id=1, replica_groups=mesh['line'=8,'bus'=32] {'line','bus'}, use_global_device_ids=true, to_apply=%region_9.10 | all-reduce | flops 64 | bytes 512 | tf_op jit(solution)/shard_map/psum | solution.py:68
  1049.5 0.5 broadcast_multiply_fusion.1
  1050.0 0.0 all-reduce.12.cloned.1.call-done
  1050.0 1.5 constant_dynamic-slice_fusion
  (19 shorter events, 0.3 us)
Async XLA Ops:
  7.2 1.1 copy-start
  7.2 395.8 %copy-start.3 = (s32[256]{0:T(256)S(1)}, s32[256]{0:T(256)}, u32[]{:S(2)}) copy-start(s32[256]{0:T(256)} %param.11) | copy-start | bytes 3076
  7.2 395.8 %copy-start.2 = (s32[4,512]{1,0:T(4,128)S(1)}, s32[4,512]{1,0:T(4,128)}, u32[]{:S(2)}) copy-start(s32[4,512]{1,0:T(4,128)} %param.12) | copy-start | bytes 24580
  7.2 395.8 %copy-start.4 = (s32[64]{0:T(128)S(1)}, s32[64]{0:T(128)}, u32[]{:S(2)}) copy-start(s32[64]{0:T(128)} %param.13) | copy-start | bytes 772
  7.2 448.4 %copy-start.1 = (f32[512,256]{1,0:T(8,128)S(1)}, f32[512,256]{1,0:T(8,128)}, u32[]{:S(2)}) copy-start(f32[512,256]{1,0:T(8,128)} %param.10) | copy-start | bytes 1572868
  7.2 395.6 %all-reduce.6.cloned.1.call-start = ((), (), s32[]{:S(2)}) async-start(), calls=%async_computation | async-start | bytes 262144 | tf_op jit(solution)/shard_map/psum | solution.py:21
  15.5 437.5 %all-gather.2.cloned.1.call-start = ((), (), s32[]{:S(2)}) async-start(), calls=%async_computation.1 | async-start | bytes 1179648 | tf_op jit(solution)/shard_map/all_gather | solution.py:27
  402.9 161.6 %all-reduce.8.cloned.1.call-start = ((), (), s32[]{:S(2)}) async-start(), calls=%async_computation.2 | async-start | bytes 131072 | tf_op jit(solution)/shard_map/psum | solution.py:63
  496.1 461.5 %copy-start.5 = (u32[256]{0:T(256)S(1)}, u32[256]{0:T(256)}, u32[]{:S(2)}) copy-start(u32[256]{0:T(256)} %constant.60) | copy-start | bytes 3076
  496.2 455.5 %all-reduce.10.cloned.1.call-start = ((), (), s32[]{:S(2)}) async-start(), calls=%async_computation.3 | async-start | bytes 262144 | tf_op jit(solution)/shard_map/psum | solution.py:67
  566.5 483.5 %all-reduce.12.cloned.1.call-start = ((), (), s32[]{:S(2)}) async-start(), calls=%async_computation.4 | async-start | bytes 1114112
Sparse Core Ops, SparseCore 0:
  15.6 387.1 all-reduce.5
  404.8 48.1 all-gather.1
  496.3 68.2 all-reduce.7
  567.0 384.6 all-reduce.9
  957.7 82.9 all-reduce.11
where the time goes:
time: 1060 us
  waiting for transfers between devices  890 us (84%)
  blocking collectives  90.6 us (9%)
  other arithmetic  32.9 us (3%)
  matrix products  15.4 us (1%)
  between operations  14.6 us (1%)
  local copies, waits for them, and re-layouts  13.9 us (1%)
    psum x1, waiting for transfers between devices, body(): line_flows = lax.psum(partial_flows, 'bus')  387 us
    psum x1, waiting for transfers between devices, body(): flow_grad, penalty_sum = lax.psum((direct + carried, penalty), 'bus')  385 us
    psum x1, blocking collectives, body(): total_penalty = lax.psum(penalty, ('line', 'bus'))  90.6 us
    psum x1, waiting for transfers between devices, body(): back = lax.psum(back_part, 'line')  68.3 us
    all_gather x1, waiting for transfers between devices, body(): every_flow = lax.all_gather(line_flows, 'line', axis=1, tiled=True)  49.7 us
    reduce_sum x4, other arithmetic, one_block(): jnp.sum(weight * outage_factors[None, :, :], axis=1)  32.2 us
  transfers between devices with their start and end apart: 5, of which 4 were waited for; matrix products, arithmetic and copies ran while one was open for 0% of the time, Pallas kernels for 0%

commit v1 on v0

--- a/solution.py
+++ b/solution.py
@@ -65,7 +65,7 @@
         back, selector.T, precision=lax.Precision.HIGHEST, preferred_element_type=jnp.float32
     )
     flow_grad, penalty_sum = lax.psum((direct + carried, penalty), "bus")
-    total_penalty = lax.psum(penalty, ("line", "bus"))
+    total_penalty = lax.psum(lax.psum(penalty, "line"), "bus")
     mean_penalty = total_penalty / (LINES * OUTAGES)
     injection_grad = lax.psum_scatter(
         jnp.dot(

time: 1060 us -> 1110 us (1.047)
  blocking collectives: 90.6 us -> 131 us
    psum x1 -> x2, blocking collectives: 90.6 us -> 131 us  [body(): total_penalty = lax.psum(lax.psum(penalty, 'line'), 'bus')]
where the time goes in v1:
time: 1110 us; the launch traced here: 1100 us
  waiting for transfers between devices  890 us (80%)
  blocking collectives  131 us (12%)
  other arithmetic  32.9 us (3%)
  matrix products  15.4 us (1%)
  between operations  14.6 us (1%)
  local copies, waits for them, and re-layouts  13.9 us (1%)
    psum x1, waiting for transfers between devices, body(): line_flows = lax.psum(partial_flows, 'bus')  387 us
    psum x1, waiting for transfers between devices, body(): flow_grad, penalty_sum = lax.psum((direct + carried, penalty), 'bus')  385 us
    psum x2, blocking collectives, body(): total_penalty = lax.psum(lax.psum(penalty, 'line'), 'bus')  131 us
    psum x1, waiting for transfers between devices, body(): back = lax.psum(back_part, 'line')  68.3 us
    all_gather x1, waiting for transfers between devices, body(): every_flow = lax.all_gather(line_flows, 'line', axis=1, tiled=True)  49.7 us
    reduce_sum x4, other arithmetic, one_block(): jnp.sum(weight * outage_factors[None, :, :], axis=1)  32.2 us
  transfers between devices with their start and end apart: 5, of which 4 were waited for; matrix products, arithmetic and copies ran while one was open for 0% of the time, Pallas kernels for 0%

profile of v1, /device:TPU:1, one launch (start us, length us, event | category | flops | bytes accessed | tf_op | source)
XLA Modules:
  0.0 1098.7 jit_solution(1437275878230840018)
XLA Ops:
  7.2 0.0 copy-start
  7.2 0.0 copy-start.3
  7.2 0.0 copy-start.2
  7.2 0.0 copy-start.4
  7.2 0.0 copy-start.1
  7.2 0.0 all-reduce.6.cloned.1.call-start
  7.3 1.0 copy-done
  8.2 7.3 fusion.3
  15.5 0.0 all-reduce.6.cloned.1.call-update
  15.5 0.0 all-gather.2.cloned.1.call-start
  15.6 387.3 %all-reduce.6.cloned.1.call-done = f32[64,512]{1,0:T(8,128)} async-done(((f32[64,512]{1,0:T(8,128)}), f32[64,512]{1,0:T(8,128)}) %all-reduce.6.cloned.1.call-update) | async-done | bytes 131088 | tf_op jit(solution)/shard_map/psum | solution.py:21
  402.9 0.0 all-gather.2.cloned.1.call-update
  402.9 0.0 all-reduce.8.cloned.1.call-start
  403.0 0.0 copy-done.3
  403.0 0.0 copy-done.2
  403.0 0.0 copy-done.4
  403.0 0.2 convolution_multiply_fusion
  403.3 49.7 %all-gather.2.cloned.1.call-done = f32[64,4096]{1,0:T(8,128)} async-done(((f32[64,512]{1,0:T(8,128)}), f32[64,4096]{1,0:T(8,128)}) %all-gather.2.cloned.1.call-update) | async-done | bytes 1048592 | tf_op jit(solution)/shard_map/all_gather | solution.py:27
  453.0 1.8 copy.14
  454.8 0.7 gather_fusion
  455.6 0.1 copy.15
  455.7 0.0 copy-done.1
  455.7 40.5 %while.14 = (s32[]{:T(128)}, f32[4,16]{1,0:T(4,128)S(1)}, f32[4,16,512]{2,1,0:T(8,128)}, f32[4,16,256]{2,1,0:T(8,128)}, f32[4,16,512]{2,1,0:T(8,128)}, /*index=5...) while((s32[]{:T(128)}, f32[4,16]{1,0:T(4,128)S(1)}, ...), condition=%wide.region_5.6_spmd, body=%wide.region_1.5_spmd.sunk | while | flops 29478896 | bytes 2491697 | solution.py:52
  455.7 0.8 dynamic-slice_bitcast_fusion.5
  456.5 8.0 multiply_reduce_fusion.4
  464.5 0.6 bitcast_dynamic-update-slice_fusion.4
  465.1 0.6 bitcast_dynamic-update-slice_fusion.5
  465.8 0.8 dynamic-slice_bitcast_fusion.5
  466.6 8.0 multiply_reduce_fusion.4
  474.6 0.6 bitcast_dynamic-update-slice_fusion.4
  475.3 0.6 bitcast_dynamic-update-slice_fusion.5
  475.9 0.8 dynamic-slice_bitcast_fusion.5
  476.7 8.0 multiply_reduce_fusion.4
  484.8 0.6 bitcast_dynamic-update-slice_fusion.4
  485.4 0.6 bitcast_dynamic-update-slice_fusion.5
  486.0 0.8 dynamic-slice_bitcast_fusion.5
  486.8 8.0 multiply_reduce_fusion.4
  494.9 0.6 bitcast_dynamic-update-slice_fusion.4
  495.5 0.6 bitcast_dynamic-update-slice_fusion.5
  496.1 0.0 copy-start.5
  496.1 0.0 all-reduce.8.cloned.1.call-update
  496.2 0.0 all-reduce.10.cloned.1.call-start
  496.2 68.3 %all-reduce.8.cloned.1.call-done = f32[64,256]{1,0:T(8,128)} async-done(((f32[64,256]{1,0:T(8,128)}), f32[64,256]{1,0:T(8,128)}) %all-reduce.8.cloned.1.call-update) | async-done | bytes 65552 | tf_op jit(solution)/shard_map/psum | solution.py:63
  564.5 2.0 convolution_add_fusion
  566.5 0.0 all-reduce.10.cloned.1.call-update
  566.5 0.0 all-reduce.12.cloned.1.call-start
  566.6 385.1 %all-reduce.10.cloned.1.call-done = f32[64,512]{1,0:T(8,128)} async-done(((f32[64,512]{1,0:T(8,128)}), f32[64,512]{1,0:T(8,128)}) %all-reduce.10.cloned.1.call-update) | async-done | bytes 131088 | tf_op jit(solution)/shard_map/psum | solution.py:67
  951.7 5.9 fusion.4
  957.5 0.0 all-reduce.12.cloned.1.call-update
  957.6 0.0 copy-done.5
  957.6 0.6 dynamic-slice
  958.8 0.1 reshape.44
  958.9 31.8 %psum.38 = f32[64]{0:T(128)S(1)} all-reduce(f32[64]{0:T(128)S(1)} %reshape.44), channel_id=1, replica_groups=mesh['line'=8,'bus'=32] {'line'}, use_global_device_ids=true, to_apply=%region_9.10 | all-reduce | flops 64 | bytes 512 | tf_op jit(solution)/shard_map/psum | solution.py:68
  990.7 99.4 %psum.39 = f32[64]{0:T(128)S(1)} all-reduce(f32[64]{0:T(128)S(1)} %psum.38), channel_id=1, replica_groups=mesh['line'=8,'bus'=32] {'bus'}, use_global_device_ids=true, to_apply=%region_10.11 | all-reduce | flops 64 | bytes 512 | tf_op jit(solution)/shard_map/psum | solution.py:68
  1090.1 0.5 broadcast_multiply_fusion.1
  1090.6 0.0 all-reduce.12.cloned.1.call-done
  1090.6 1.5 constant_dynamic-slice_fusion
  (19 shorter events, 0.3 us)
Async XLA Ops:
  7.2 1.1 copy-start
  7.2 395.8 %copy-start.3 = (s32[256]{0:T(256)S(1)}, s32[256]{0:T(256)}, u32[]{:S(2)}) copy-start(s32[256]{0:T(256)} %param.11) | copy-start | bytes 3076
  7.2 395.8 %copy-start.2 = (s32[4,512]{1,0:T(4,128)S(1)}, s32[4,512]{1,0:T(4,128)}, u32[]{:S(2)}) copy-start(s32[4,512]{1,0:T(4,128)} %param.12) | copy-start | bytes 24580
  7.2 395.8 %copy-start.4 = (s32[64]{0:T(128)S(1)}, s32[64]{0:T(128)}, u32[]{:S(2)}) copy-start(s32[64]{0:T(128)} %param.13) | copy-start | bytes 772
  7.2 448.5 %copy-start.1 = (f32[512,256]{1,0:T(8,128)S(1)}, f32[512,256]{1,0:T(8,128)}, u32[]{:S(2)}) copy-start(f32[512,256]{1,0:T(8,128)} %param.10) | copy-start | bytes 1572868
  7.2 395.6 %all-reduce.6.cloned.1.call-start = ((), (), s32[]{:S(2)}) async-start(), calls=%async_computation | async-start | bytes 262144 | tf_op jit(solution)/shard_map/psum | solution.py:21
  15.5 437.5 %all-gather.2.cloned.1.call-start = ((), (), s32[]{:S(2)}) async-start(), calls=%async_computation.1 | async-start | bytes 1179648 | tf_op jit(solution)/shard_map/all_gather | solution.py:27
  402.9 161.6 %all-reduce.8.cloned.1.call-start = ((), (), s32[]{:S(2)}) async-start(), calls=%async_computation.2 | async-start | bytes 131072 | tf_op jit(solution)/shard_map/psum | solution.py:63
  496.1 461.4 %copy-start.5 = (u32[256]{0:T(256)S(1)}, u32[256]{0:T(256)}, u32[]{:S(2)}) copy-start(u32[256]{0:T(256)} %constant.60) | copy-start | bytes 3076
  496.2 455.5 %all-reduce.10.cloned.1.call-start = ((), (), s32[]{:S(2)}) async-start(), calls=%async_computation.3 | async-start | bytes 262144 | tf_op jit(solution)/shard_map/psum | solution.py:67
  566.5 524.1 %all-reduce.12.cloned.1.call-start = ((), (), s32[]{:S(2)}) async-start(), calls=%async_computation.4 | async-start | bytes 1114112
Sparse Core Ops, SparseCore 0:
  15.6 387.1 all-reduce.5
  404.8 48.1 all-gather.1
  496.3 68.2 all-reduce.7
  567.0 384.6 all-reduce.9
  957.7 83.3 all-reduce.11
